TPU v7x, 32 devices: a whole 2x2x4 slice. The times are simulated.
32 devices in a mesh: sample: 2 (over core), sx: 4 (over y, x), sy: 4 (over z).
Axes of the slice: x: 2, y: 2, z: 4, core: 2. Of those that a mesh axis runs over, the one named last changes fastest.
Arguments:
- features: bfloat16 [16, 4, 16, 32, 256], P('sx', 'sample', 'sy'), may hold values from -6 to 6
- kernel: bfloat16 [3, 3, 3, 256, 256], P(None, None, None, 'sx', 'sy'), may hold values from -0.078125 to 0.078125
- filter_bias: bfloat16 [256], P('sy'), may hold values from -3 to 3
- cotangent: bfloat16 [16, 4, 16, 32, 256], P('sx', 'sample', None, None, 'sy'), may hold values from -6 to 6
Outputs:
- output: bfloat16 [16, 4, 16, 32, 256], P('sx', 'sample', None, None, 'sy')
- input_grad: bfloat16 [16, 4, 16, 32, 256], P('sx', 'sample', 'sy')
- kernel_grad: float32 [3, 3, 3, 256, 256], P(None, None, None, 'sx', 'sy')
All inputs are finite; a program needn't handle non-finite values.
Results may differ from a plain program's by a relative error of at most 0.014.
Values may be sent and summed in bfloat16 or wider, within the bound.
A program may use at most 128 MiB of HBM per device.

v0:
```python
import jax
import jax.numpy as jnp
from jax import lax
from jax.sharding import PartitionSpec as P


def padded_2(array, sides, width):
    for axis, dim in sides:
        size, length = (lax.axis_size(axis), array.shape[dim])
        up = [(i, (i + 1) % size) for i in range(size - 1)]
        down = [(j, i) for i, j in up]
        last = lax.slice_in_dim(array, length - width, length, axis=dim)
        leading = lax.slice_in_dim(array, 0, width, axis=dim)
        before = lax.ppermute(last, axis, up)
        after = lax.ppermute(leading, axis, down)
        array = jnp.concatenate([before, array, after], axis=dim)
    return array


def slope_of(hidden):
    gate = jax.nn.sigmoid(hidden)
    return gate * (1.0 + hidden * (1.0 - gate))


def convolve(inputs, weights, pads, layout):
    return lax.conv_general_dilated(
        inputs,
        weights,
        (1, 1, 1),
        pads,
        dimension_numbers=layout,
        preferred_element_type=jnp.float32,
    )


def forward_conv(inputs, weights):
    return convolve(inputs, weights, ((0, 0), (0, 0), (0, 0)), ("DNHWC", "DHWIO", "DNHWC"))


def kernel_grad_of(window, grad_pre):
    return convolve(window, grad_pre, ((0, 0), (0, 0), (0, 0)), ("DCHWN", "DIHWO", "DHWNC"))


def local(features, kernel, filter_bias, cotangent):
    kernel_full = lax.all_gather(kernel, "sx", axis=3, tiled=True)
    edged = padded_2(features, (("sx", 0),), 1)
    band = lax.all_gather(edged, "sy", axis=2, tiled=True)
    padded = jnp.pad(band, ((0, 0), (0, 0), (1, 1), (1, 1), (0, 0)))
    hidden = forward_conv(padded, kernel_full) + filter_bias.astype(jnp.float32)
    output = jax.nn.silu(hidden).astype(jnp.bfloat16)
    grad_pre = (cotangent.astype(jnp.float32) * slope_of(hidden)).astype(jnp.bfloat16)
    grad_band = padded_2(grad_pre, (("sx", 0),), 1)
    grad_padded = jnp.pad(grad_band, ((0, 0), (0, 0), (1, 1), (1, 1), (0, 0)))
    flipped = kernel_full[::-1, ::-1, ::-1]
    partial_grad = convolve(
        grad_padded, flipped, ((0, 0), (0, 0), (0, 0)), ("DNHWC", "DHWOI", "DNHWC")
    )
    input_grad = lax.psum_scatter(
        partial_grad.astype(jnp.bfloat16), "sy", scatter_dimension=2, tiled=True
    )
    local_grad = kernel_grad_of(padded, grad_pre)
    weight_sum = lax.psum_scatter(
        local_grad.astype(jnp.bfloat16), "sx", scatter_dimension=3, tiled=True
    )
    kernel_grad = lax.psum(weight_sum, "sample").astype(jnp.float32)
    return (output, input_grad, kernel_grad)


def solution(mesh):
    return jax.shard_map(
        local,
        mesh=mesh,
        in_specs=(
            P("sx", "sample", "sy", None, None),
            P(None, None, None, "sx", "sy"),
            P("sy"),
            P("sx", "sample", None, None, "sy"),
        ),
        out_specs=(
            P("sx", "sample", None, None, "sy"),
            P("sx", "sample", "sy", None, None),
            P(None, None, None, "sx", "sy"),
        ),
        check_vma=False,
    )
```

profile of v0, /device:TPU:0, one launch (start us, length us, event | category | flops | bytes accessed | tf_op | source)
XLA Modules:
  0.0 269.2 jit_solution(10570267025638348491)
XLA Ops:
  7.2 1.6 copy.28
  9.1 4.9 %collective-permute-start = (bf16[1,2,4,32,256]{4,1,3,2,0:T(2,128)(2,1)S(1)}, bf16[1,2,4,32,256]{4,1,3,2,0:T(2,128)(2,1)S(1)}, u32[]{:S(2)}, u32[]{:S(2)}) collective-permute-start(bf16[1,2,4,32,256]{4,1,3,2,0:T(2,128)(2,1)S(1)} %get-tuple-element.13), channel_id=1, source_target_pairs={{0,4},{4,8},{8,12},{1,5},{5,9},{9,13},{2,6},{6,10},{10,14},{3,7},{... | collective-permute-start | bytes 393224 | tf_op jit(solution)/shard_map/ppermute | solution.py:14
  13.9 1.3 collective-permute-start.1
  15.2 1.4 collective-permute-done
  16.7 4.8 %collective-permute-done.1 = bf16[1,2,4,32,256]{4,1,3,2,0:T(2,128)(2,1)S(1)} collective-permute-done((bf16[1,2,4,32,256]{4,1,3,2,0:T(2,128)(2,1)S(1)}, bf16[1,2,4,32,256]{4,1,3,2,0:T(2,128)(2,1)S(1)}, u32[]{:S(2)}, u32[]{:S(2)}) %collective-permute-start.1) | collective-permute-done | bytes 131104 | tf_op jit(solution)/shard_map/ppermute | solution.py:15
  21.4 2.1 pad_maximum_fusion
  23.6 17.6 %all_gather.7 = bf16[3,3,3,256,64]{4,3,2,1,0:T(8,128)(2,1)S(1)} all-gather(bf16[3,3,3,64,64]{4,3,2,1,0:T(8,128)(2,1)S(1)} %copy-done.5), channel_id=1, replica_groups=mesh['sample'=2,'sx'=4,'sy'=4] {'sx'}, dimensions={3}, use_global_device_ids=true | all-gather | bytes 1105920 | tf_op jit(solution)/shard_map/all_gather | solution.py:45
  41.2 46.4 %all-gather.2.cloned.1.call-done = bf16[6,2,16,32,256]{4,1,3,2,0:T(2,128)(2,1)} async-done(((bf16[6,2,4,32,256]{4,1,3,2,0:T(2,128)(2,1)}), bf16[6,2,16,32,256]{4,1,3,2,0:T(2,128)(2,1)}) %all-gather.2.cloned.1.call-update) | async-done | bytes 3145744 | tf_op jit(solution)/shard_map/all_gather | solution.py:47
  87.7 4.8 %pad.4 = bf16[6,16,2,40,256]{4,2,3,1,0:T(2,128)(2,1)S(1)} pad(bf16[6,16,2,32,256]{4,2,3,1,0:T(2,128)(2,1)} %bitcast.37, bf16[]{:T(256)} %constant.6), padding=0_0x0_0x0_0x1_7x0_0 | pad | bytes 7077890 | tf_op jit(solution)/shard_map/all_gather | solution.py:47
  92.5 0.8 copy.32
  93.3 0.4 slice.23
  94.0 21.8 %add_multiply_fusion = (f32[4,16,16,5,64]{4,2,3,1,0:T(8,128)S(1)}, bf16[4,16,16,5,64]{4,2,3,1,0:T(8,128)(2,1)}) fusion(f32[64]{0:T(128)S(1)} %convert_element_type.25, pred[16,5]{0,1:T(8,128)(4,1)S(1)} %copy-done.7, bf16[3,3,3,256,64]{4,3,2,1,0:T(8,128)(2,1)S(1)} %all_gather.7, bf16[6,16,2,7,2,256]{5,3,2,4,1,0:T(8,128)(2,1)S(1)} %slice.23, ...), kind=kOutput, calls=%fused_computation.16 | convolution fusion | flops 4361224192 | bytes 8159568 | tf_op jit(solution)/shard_map/conv_general_dilated | solution.py:26
  115.8 0.8 copy.35
  116.6 0.4 copy-done.4
  117.1 0.5 fusion.15
  117.6 0.8 fusion.22
  118.4 4.1 %collective-permute-start.2 = (bf16[1,2,16,32,64]{4,2,3,1,0:T(8,128)(2,1)}, bf16[1,2,16,32,64]{4,2,3,1,0:T(8,128)(2,1)}, u32[]{:S(2)}, u32[]{:S(2)}) collective-permute-start(bf16[1,2,16,32,64]{4,2,3,1,0:T(8,128)(2,1)} %get-tuple-element.11), channel_id=1, source_target_pairs={{0,4},{4,8},{8,12},{1,5},{5,9},{9,13},{2,6},{6,10},{10,14},{3,7},{... | collective-permute-start | bytes 393224 | tf_op jit(solution)/shard_map/ppermute | solution.py:14
  122.5 1.3 collective-permute-start.3
  123.8 36.4 %convolution_convert_fusion = bf16[3,3,3,256,64]{4,3,2,1,0:T(8,128)(2,1)} fusion(bf16[6,2,16,32,256]{4,1,3,2,0:T(2,128)(2,1)S(1)} %copy-done, bf16[4,2,16,32,64]{4,2,3,1,0:T(8,128)(2,1)S(1)} %fusion.15), kind=kOutput, calls=%fused_computation.24 | convolution fusion | flops 3400974336 | bytes 4554752 | tf_op jit(solution)/shard_map/conv_general_dilated | solution.py:26
  160.3 1.4 maximum_bitcast_fusion
  161.7 0.4 pad.6
  162.3 0.7 fusion.9
  163.0 0.8 copy-done.2
  163.8 10.1 %select_convert_fusion = bf16[4,16,16,5,256]{4,2,3,1,0:T(8,128)(2,1)S(1)} fusion(pred[16,5]{0,1:T(8,128)(4,1)S(1)} %copy-done.8, bf16[3,3,3,256,64]{4,3,2,1,0:T(8,128)(2,1)S(1)} %copy-done.2, bf16[6,16,2,8,7,64]{5,1,4,3,2,0:T(8,128)(2,1)S(1)} %fusion.9), kind=kOutput, calls=%fused_computation.10 | convolution fusion | flops 4343726080 | bytes 4882512 | tf_op jit(solution)/shard_map/conv_general_dilated | solution.py:26
  173.8 1.0 copy.37
  174.8 17.9 %reduce-scatter.5.cloned.1.call-done = bf16[3,3,3,64,64]{4,3,2,1,0:T(8,128)(2,1)} async-done(((bf16[3,3,3,256,64]{4,3,2,1,0:T(8,128)(2,1)}), bf16[3,3,3,64,64]{4,3,2,1,0:T(8,128)(2,1)}) %reduce-scatter.5.cloned.1.call-update) | async-done | bytes 221200 | tf_op jit(solution)/shard_map/reduce_scatter | solution.py:62
  193.0 2.1 copy.38
  195.6 1.2 copy.40
  196.9 16.7 %all-reduce.2.cloned.1.call-done = bf16[3,3,3,64,64]{4,3,2,1,0:T(8,128)(2,1)} async-done(((bf16[3,3,3,64,64]{4,3,2,1,0:T(8,128)(2,1)}), bf16[3,3,3,64,64]{4,3,2,1,0:T(8,128)(2,1)}) %all-reduce.2.cloned.1.call-update) | async-done | bytes 221200 | tf_op jit(solution)/shard_map/psum | solution.py:65
  213.6 2.0 convert_element_type.31
  215.6 45.0 %reduce-scatter.3.cloned.1.call-done = bf16[4,2,4,32,256]{4,3,1,0,2:T(8,128)(2,1)} async-done(((bf16[4,2,16,32,256]{4,3,1,0,2:T(8,128)(2,1)}), bf16[4,2,4,32,256]{4,3,1,0,2:T(8,128)(2,1)}) %reduce-scatter.3.cloned.1.call-update) | async-done | bytes 524304 | tf_op jit(solution)/shard_map/reduce_scatter | solution.py:58
  260.6 1.9 copy.41
  (32 shorter events, 1.5 us)
Async XLA Ops:
  7.2 16.4 %copy-start.6 = (bf16[64]{0:T(256)(128)(2,1)S(1)}, bf16[64]{0:T(256)(128)(2,1)}, u32[]{:S(2)}) copy-start(bf16[64]{0:T(256)(128)(2,1)} %param.6) | copy-start | bytes 388
  7.2 16.4 %copy-start.5 = (bf16[3,3,3,64,64]{4,3,2,1,0:T(8,128)(2,1)S(1)}, bf16[3,3,3,64,64]{4,3,2,1,0:T(8,128)(2,1)}, u32[]{:S(2)}) copy-start(bf16[3,3,3,64,64]{4,3,2,1,0:T(8,128)(2,1)} %param.5) | copy-start | bytes 663556
  7.2 80.5 %all-gather.2.cloned.1.call-start = ((), (), s32[]{:S(2)}) async-start(), calls=%async_computation.2 | async-start | bytes 3932160 | tf_op jit(solution)/shard_map/all_gather | solution.py:47
  9.1 7.6 %collective-permute-start = (bf16[1,2,4,32,256]{4,1,3,2,0:T(2,128)(2,1)S(1)}, bf16[1,2,4,32,256]{4,1,3,2,0:T(2,128)(2,1)S(1)}, u32[]{:S(2)}, u32[]{:S(2)}) collective-permute-start(bf16[1,2,4,32,256]{4,1,3,2,0:T(2,128)(2,1)S(1)} %get-tuple-element.13), channel_id=1, source_target_pairs={{0,4},{4,8},{8,12},{1,5},{5,9},{9,13},{2,6},{6,10},{10,14},{3,7},{... | collective-permute-start | bytes 393224 | tf_op jit(solution)/shard_map/ppermute | solution.py:14
  13.9 7.5 %collective-permute-start.1 = (bf16[1,2,4,32,256]{4,1,3,2,0:T(2,128)(2,1)S(1)}, bf16[1,2,4,32,256]{4,1,3,2,0:T(2,128)(2,1)S(1)}, u32[]{:S(2)}, u32[]{:S(2)}) collective-permute-start(bf16[1,2,4,32,256]{4,1,3,2,0:T(2,128)(2,1)S(1)} %get-tuple-element.14), channel_id=1, source_target_pairs={{4,0},{8,4},{12,8},{5,1},{9,5},{13,9},{6,2},{10,6},{14,10},{7,3},{... | collective-permute-start | bytes 393224 | tf_op jit(solution)/shard_map/ppermute | solution.py:15
  23.5 169.2 %reduce-scatter.5.cloned.1.call-start = ((), (), s32[]{:S(2)}) async-start(), calls=%async_computation.4 | async-start | bytes 2211840 | tf_op jit(solution)/shard_map/reduce_scatter | solution.py:62
  41.2 52.5 %copy-start.1 = (bf16[3,3,3,256,64]{4,3,2,1,0:T(8,128)(2,1)}, bf16[3,3,3,256,64]{4,3,2,1,0:T(8,128)(2,1)S(1)}, u32[]{:S(2)}) copy-start(bf16[3,3,3,256,64]{4,3,2,1,0:T(8,128)(2,1)S(1)} %all_gather.7) | copy-start | bytes 2654212
  93.3 0.7 copy-start.7
  115.8 1.2 copy-start.4
  117.1 6.7 %copy-start = (bf16[6,2,16,32,256]{4,1,3,2,0:T(2,128)(2,1)S(1)}, bf16[6,2,16,32,256]{4,1,3,2,0:T(2,128)(2,1)}, u32[]{:S(2)}) copy-start(bf16[6,2,16,32,256]{4,1,3,2,0:T(2,128)(2,1)} %all-gather.2.cloned.1.call-done) | copy-start | bytes 9437188
  118.4 41.9 %collective-permute-start.2 = (bf16[1,2,16,32,64]{4,2,3,1,0:T(8,128)(2,1)}, bf16[1,2,16,32,64]{4,2,3,1,0:T(8,128)(2,1)}, u32[]{:S(2)}, u32[]{:S(2)}) collective-permute-start(bf16[1,2,16,32,64]{4,2,3,1,0:T(8,128)(2,1)} %get-tuple-element.11), channel_id=1, source_target_pairs={{0,4},{4,8},{8,12},{1,5},{5,9},{9,13},{2,6},{6,10},{10,14},{3,7},{... | collective-permute-start | bytes 393224 | tf_op jit(solution)/shard_map/ppermute | solution.py:14
  122.5 37.8 %collective-permute-start.3 = (bf16[1,2,16,32,64]{4,2,3,1,0:T(8,128)(2,1)}, bf16[1,2,16,32,64]{4,2,3,1,0:T(8,128)(2,1)}, u32[]{:S(2)}, u32[]{:S(2)}) collective-permute-start(bf16[1,2,16,32,64]{4,2,3,1,0:T(8,128)(2,1)} %get-tuple-element.12), channel_id=1, source_target_pairs={{4,0},{8,4},{12,8},{5,1},{9,5},{13,9},{6,2},{10,6},{14,10},{7,3},{... | collective-permute-start | bytes 393224 | tf_op jit(solution)/shard_map/ppermute | solution.py:15
  160.3 53.3 %all-reduce.2.cloned.1.call-start = ((), (), s32[]{:S(2)}) async-start(), calls=%async_computation.5 | async-start | bytes 884736 | tf_op jit(solution)/shard_map/psum | solution.py:65
  162.3 1.5 copy-start.2
  162.3 1.5 copy-start.8
  192.7 67.9 %reduce-scatter.3.cloned.1.call-start = ((), (), s32[]{:S(2)}) async-start(), calls=%async_computation.3 | async-start | bytes 2621440 | tf_op jit(solution)/shard_map/reduce_scatter | solution.py:58
  193.0 2.1 copy-start.3
Sparse Core Ops, SparseCore 0:
  23.6 63.9 all-gather.1
  160.4 32.2 reduce-scatter.4
  195.0 18.4 all-reduce.1
  215.7 44.8 reduce-scatter.2
where the time goes:
time: 272 us; the launch traced here: 269 us
  waiting for transfers between devices  132 us (49%)
  matrix products  68.3 us (25%)
  local copies, waits for them, and re-layouts  18.4 us (7%)
  blocking collectives  17.6 us (6%)
  between operations  14.2 us (5%)
  starting transfers between devices  11.7 us (4%)
  other arithmetic  6.64 us (2%)
    conv_general_dilated x3, matrix products, convolve(): lax.conv_general_dilated(inputs, weights, (1, 1, 1), pads, dimension_numb...  68.3 us
    all_gather x1, waiting for transfers between devices, local(): band = lax.all_gather(edged, 'sy', axis=2, tiled=True)  46.4 us
    reduce_scatter x1, waiting for transfers between devices, local(): lax.psum_scatter(partial_grad.astype(jnp.bfloat16), 'sy', scatter_dimensi...  45 us
    reduce_scatter x1, waiting for transfers between devices, local(): lax.psum_scatter(local_grad.astype(jnp.bfloat16), 'sx', scatter_dimension...  17.9 us
    all_gather x1, blocking collectives, local(): kernel_full = lax.all_gather(kernel, 'sx', axis=3, tiled=True)  17.6 us
    psum x1, waiting for transfers between devices, local(): kernel_grad = lax.psum(weight_sum, 'sample').astype(jnp.float32)  16.7 us
    ppermute x2, starting transfers between devices, padded_2(): before = lax.ppermute(last, axis, up)  8.97 us
    unnamed x21, local copies, waits for them, and re-layouts  6.24 us
  transfers between devices with their start and end apart: 8, of which 6 were waited for; matrix products, arithmetic and copies ran while one was open for 21% of the time, Pallas kernels for 0%

commit v1 on v0

--- a/solution.py
+++ b/solution.py
@@ -62,7 +62,7 @@
     weight_sum = lax.psum_scatter(
         local_grad.astype(jnp.bfloat16), "sx", scatter_dimension=3, tiled=True
     )
-    kernel_grad = lax.psum(weight_sum, "sample").astype(jnp.float32)
+    kernel_grad = jnp.sum(lax.all_gather(weight_sum, "sample"), axis=0).astype(jnp.float32)
     return (output, input_grad, kernel_grad)
 
 

time: 272 us -> 250 us (0.919)
  waiting for transfers between devices: 132 us -> 109 us
    psum x1 -> x0, waiting for transfers between devices: 16.7 us -> none  [local(): kernel_grad = lax.psum(weight_sum, 'sample').astype(jnp.float32)]
    reduce_scatter x1, waiting for transfers between devices: 17.9 us -> 13.9 us  [local(): lax.psum_scatter(local_grad.astype(jnp.bfloat16), 'sx', scatter_dimension...]
    reduce_scatter x1, waiting for transfers between devices: 45 us -> 42.1 us  [local(): lax.psum_scatter(partial_grad.astype(jnp.bfloat16), 'sy', scatter_dimensi...]
  transfers between devices with their start and end apart: 8 -> 7, of which waited for: 6 -> 5; matrix products, arithmetic and copies ran while one was open for 21% -> 22% of each run, Pallas kernels for 0% -> 0%
where the time goes in v1:
time: 250 us; the launch traced here: 247 us
  waiting for transfers between devices  109 us (44%)
  matrix products  68.3 us (27%)
  blocking collectives  20.3 us (8%)
  local copies, waits for them, and re-layouts  18.3 us (7%)
  between operations  14.2 us (6%)
  starting transfers between devices  11.6 us (5%)
  other arithmetic  5.86 us (2%)
    conv_general_dilated x3, matrix products, convolve(): lax.conv_general_dilated(inputs, weights, (1, 1, 1), pads, dimension_numb...  68.3 us
    all_gather x1, waiting for transfers between devices, local(): band = lax.all_gather(edged, 'sy', axis=2, tiled=True)  46.4 us
    reduce_scatter x1, waiting for transfers between devices, local(): lax.psum_scatter(partial_grad.astype(jnp.bfloat16), 'sy', scatter_dimensi...  42.1 us
    all_gather x1, blocking collectives, local(): kernel_full = lax.all_gather(kernel, 'sx', axis=3, tiled=True)  17.6 us
    reduce_scatter x1, waiting for transfers between devices, local(): lax.psum_scatter(local_grad.astype(jnp.bfloat16), 'sx', scatter_dimension...  13.9 us
    ppermute x2, starting transfers between devices, padded_2(): before = lax.ppermute(last, axis, up)  8.95 us
    unnamed x21, local copies, waits for them, and re-layouts  6.24 us
  transfers between devices with their start and end apart: 7, of which 5 were waited for; matrix products, arithmetic and copies ran while one was open for 22% of the time, Pallas kernels for 0%

profile of v1, /device:TPU:0, one launch (start us, length us, event | category | flops | bytes accessed | tf_op | source)
XLA Modules:
  0.0 247.3 jit_solution(8904170941082912715)
XLA Ops:
  7.2 1.6 copy.28
  9.1 4.9 %collective-permute-start = (bf16[1,2,4,32,256]{4,1,3,2,0:T(2,128)(2,1)S(1)}, bf16[1,2,4,32,256]{4,1,3,2,0:T(2,128)(2,1)S(1)}, u32[]{:S(2)}, u32[]{:S(2)}) collective-permute-start(bf16[1,2,4,32,256]{4,1,3,2,0:T(2,128)(2,1)S(1)} %get-tuple-element.13), channel_id=1, source_target_pairs={{0,4},{4,8},{8,12},{1,5},{5,9},{9,13},{2,6},{6,10},{10,14},{3,7},{... | collective-permute-start | bytes 393224 | tf_op jit(solution)/shard_map/ppermute | solution.py:14
  13.9 1.3 collective-permute-start.1
  15.2 1.4 collective-permute-done
  16.7 4.8 %collective-permute-done.1 = bf16[1,2,4,32,256]{4,1,3,2,0:T(2,128)(2,1)S(1)} collective-permute-done((bf16[1,2,4,32,256]{4,1,3,2,0:T(2,128)(2,1)S(1)}, bf16[1,2,4,32,256]{4,1,3,2,0:T(2,128)(2,1)S(1)}, u32[]{:S(2)}, u32[]{:S(2)}) %collective-permute-start.1) | collective-permute-done | bytes 131104 | tf_op jit(solution)/shard_map/ppermute | solution.py:15
  21.4 2.1 pad_maximum_fusion
  23.6 17.6 %all_gather.13 = bf16[3,3,3,256,64]{4,3,2,1,0:T(8,128)(2,1)S(1)} all-gather(bf16[3,3,3,64,64]{4,3,2,1,0:T(8,128)(2,1)S(1)} %copy-done.5), channel_id=1, replica_groups=mesh['sample'=2,'sx'=4,'sy'=4] {'sx'}, dimensions={3}, use_global_device_ids=true | all-gather | bytes 1105920 | tf_op jit(solution)/shard_map/all_gather | solution.py:45
  41.2 46.4 %all-gather.3.cloned.1.call-done = bf16[6,2,16,32,256]{4,1,3,2,0:T(2,128)(2,1)} async-done(((bf16[6,2,4,32,256]{4,1,3,2,0:T(2,128)(2,1)}), bf16[6,2,16,32,256]{4,1,3,2,0:T(2,128)(2,1)}) %all-gather.3.cloned.1.call-update) | async-done | bytes 3145744 | tf_op jit(solution)/shard_map/all_gather | solution.py:47
  87.7 4.8 %pad.4 = bf16[6,16,2,40,256]{4,2,3,1,0:T(2,128)(2,1)S(1)} pad(bf16[6,16,2,32,256]{4,2,3,1,0:T(2,128)(2,1)} %bitcast.39, bf16[]{:T(256)} %constant.8.clone.1), padding=0_0x0_0x0_0x1_7x0_0 | pad | bytes 7077890 | tf_op jit(solution)/shard_map/all_gather | solution.py:47
  92.5 0.8 copy.32
  93.3 0.4 slice.23
  94.0 21.8 %add_multiply_fusion = (f32[4,16,16,5,64]{4,2,3,1,0:T(8,128)S(1)}, bf16[4,16,16,5,64]{4,2,3,1,0:T(8,128)(2,1)}) fusion(f32[64]{0:T(128)S(1)} %convert_element_type.27, pred[16,5]{0,1:T(8,128)(4,1)S(1)} %copy-done.7, bf16[3,3,3,256,64]{4,3,2,1,0:T(8,128)(2,1)S(1)} %all_gather.13, bf16[6,16,2,7,2,256]{5,3,2,4,1,0:T(8,128)(2,1)S(1)} %slice.23, ...), kind=kOutput, calls=%fused_computation.16 | convolution fusion | flops 4361224192 | bytes 8159568 | tf_op jit(solution)/shard_map/conv_general_dilated | solution.py:26
  115.8 0.8 copy.35
  116.6 0.4 copy-done.4
  117.0 0.5 fusion.15
  117.5 0.8 fusion.22
  118.4 4.1 %collective-permute-start.2 = (bf16[1,2,16,32,64]{4,2,3,1,0:T(8,128)(2,1)}, bf16[1,2,16,32,64]{4,2,3,1,0:T(8,128)(2,1)}, u32[]{:S(2)}, u32[]{:S(2)}) collective-permute-start(bf16[1,2,16,32,64]{4,2,3,1,0:T(8,128)(2,1)} %get-tuple-element.11), channel_id=1, source_target_pairs={{0,4},{4,8},{8,12},{1,5},{5,9},{9,13},{2,6},{6,10},{10,14},{3,7},{... | collective-permute-start | bytes 393224 | tf_op jit(solution)/shard_map/ppermute | solution.py:14
  122.4 1.3 collective-permute-start.3
  123.7 36.5 %convolution_convert_fusion = bf16[3,3,3,256,64]{4,3,2,1,0:T(8,128)(2,1)} fusion(bf16[6,2,16,32,256]{4,1,3,2,0:T(2,128)(2,1)S(1)} %copy-done, bf16[4,2,16,32,64]{4,2,3,1,0:T(8,128)(2,1)S(1)} %fusion.15), kind=kOutput, calls=%fused_computation.24 | convolution fusion | flops 3400974336 | bytes 4554752 | tf_op jit(solution)/shard_map/conv_general_dilated | solution.py:26
  160.3 1.4 maximum_bitcast_fusion
  161.7 0.4 pad.6
  162.3 0.7 fusion.9
  162.9 0.8 copy-done.2
  163.7 10.1 %select_convert_fusion = bf16[4,16,16,5,256]{4,2,3,1,0:T(8,128)(2,1)S(1)} fusion(pred[16,5]{0,1:T(8,128)(4,1)S(1)} %copy-done.8, bf16[3,3,3,256,64]{4,3,2,1,0:T(8,128)(2,1)S(1)} %copy-done.2, bf16[6,16,2,8,7,64]{5,1,4,3,2,0:T(8,128)(2,1)S(1)} %fusion.9), kind=kOutput, calls=%fused_computation.10 | convolution fusion | flops 4343726080 | bytes 4882512 | tf_op jit(solution)/shard_map/conv_general_dilated | solution.py:26
  173.8 1.0 copy.37
  174.9 2.1 copy.38
  177.6 1.2 copy.40
  178.8 13.9 %reduce-scatter.5.cloned.1.call-done = bf16[3,3,3,64,64]{4,3,2,1,0:T(8,128)(2,1)} async-done(((bf16[3,3,3,256,64]{4,3,2,1,0:T(8,128)(2,1)}), bf16[3,3,3,64,64]{4,3,2,1,0:T(8,128)(2,1)}) %reduce-scatter.5.cloned.1.call-update) | async-done | bytes 221200 | tf_op jit(solution)/shard_map/reduce_scatter | solution.py:62
  192.7 2.6 %all-gather = bf16[6,3,3,64,64]{4,3,2,1,0:T(8,128)(2,1)S(1)} all-gather(bf16[3,3,3,64,64]{4,3,2,1,0:T(8,128)(2,1)} %reduce-scatter.5.cloned.1.call-done), channel_id=2, replica_groups=mesh['sample'=2,'sx'=4,'sy'=4] {'sample'}, dimensions={0}, use_global_device_ids=true | all-gather | bytes 663552 | tf_op jit(solution)/shard_map/all_gather | solution.py:65
  195.6 1.0 convert_element_type.33
  196.6 42.1 %reduce-scatter.3.cloned.1.call-done = bf16[4,2,4,32,256]{4,3,1,0,2:T(8,128)(2,1)} async-done(((bf16[4,2,16,32,256]{4,3,1,0,2:T(8,128)(2,1)}), bf16[4,2,4,32,256]{4,3,1,0,2:T(8,128)(2,1)}) %reduce-scatter.3.cloned.1.call-update) | async-done | bytes 524304 | tf_op jit(solution)/shard_map/reduce_scatter | solution.py:58
  238.6 1.9 copy.41
  (31 shorter events, 1.6 us)
Async XLA Ops:
  7.2 16.4 %copy-start.6 = (bf16[64]{0:T(256)(128)(2,1)S(1)}, bf16[64]{0:T(256)(128)(2,1)}, u32[]{:S(2)}) copy-start(bf16[64]{0:T(256)(128)(2,1)} %param.6) | copy-start | bytes 388
  7.2 16.4 %copy-start.5 = (bf16[3,3,3,64,64]{4,3,2,1,0:T(8,128)(2,1)S(1)}, bf16[3,3,3,64,64]{4,3,2,1,0:T(8,128)(2,1)}, u32[]{:S(2)}) copy-start(bf16[3,3,3,64,64]{4,3,2,1,0:T(8,128)(2,1)} %param.5) | copy-start | bytes 663556
  7.2 80.5 %all-gather.3.cloned.1.call-start = ((), (), s32[]{:S(2)}) async-start(), calls=%async_computation.2 | async-start | bytes 3932160 | tf_op jit(solution)/shard_map/all_gather | solution.py:47
  9.1 7.6 %collective-permute-start = (bf16[1,2,4,32,256]{4,1,3,2,0:T(2,128)(2,1)S(1)}, bf16[1,2,4,32,256]{4,1,3,2,0:T(2,128)(2,1)S(1)}, u32[]{:S(2)}, u32[]{:S(2)}) collective-permute-start(bf16[1,2,4,32,256]{4,1,3,2,0:T(2,128)(2,1)S(1)} %get-tuple-element.13), channel_id=1, source_target_pairs={{0,4},{4,8},{8,12},{1,5},{5,9},{9,13},{2,6},{6,10},{10,14},{3,7},{... | collective-permute-start | bytes 393224 | tf_op jit(solution)/shard_map/ppermute | solution.py:14
  13.9 7.5 %collective-permute-start.1 = (bf16[1,2,4,32,256]{4,1,3,2,0:T(2,128)(2,1)S(1)}, bf16[1,2,4,32,256]{4,1,3,2,0:T(2,128)(2,1)S(1)}, u32[]{:S(2)}, u32[]{:S(2)}) collective-permute-start(bf16[1,2,4,32,256]{4,1,3,2,0:T(2,128)(2,1)S(1)} %get-tuple-element.14), channel_id=1, source_target_pairs={{4,0},{8,4},{12,8},{5,1},{9,5},{13,9},{6,2},{10,6},{14,10},{7,3},{... | collective-permute-start | bytes 393224 | tf_op jit(solution)/shard_map/ppermute | solution.py:15
  23.5 169.2 %reduce-scatter.5.cloned.1.call-start = ((), (), s32[]{:S(2)}) async-start(), calls=%async_computation.4 | async-start | bytes 2211840 | tf_op jit(solution)/shard_map/reduce_scatter | solution.py:62
  41.2 52.5 %copy-start.1 = (bf16[3,3,3,256,64]{4,3,2,1,0:T(8,128)(2,1)}, bf16[3,3,3,256,64]{4,3,2,1,0:T(8,128)(2,1)S(1)}, u32[]{:S(2)}) copy-start(bf16[3,3,3,256,64]{4,3,2,1,0:T(8,128)(2,1)S(1)} %all_gather.13) | copy-start | bytes 2654212
  93.3 0.7 copy-start.7
  115.8 1.2 copy-start.4
  117.0 6.7 %copy-start = (bf16[6,2,16,32,256]{4,1,3,2,0:T(2,128)(2,1)S(1)}, bf16[6,2,16,32,256]{4,1,3,2,0:T(2,128)(2,1)}, u32[]{:S(2)}) copy-start(bf16[6,2,16,32,256]{4,1,3,2,0:T(2,128)(2,1)} %all-gather.3.cloned.1.call-done) | copy-start | bytes 9437188
  118.4 41.9 %collective-permute-start.2 = (bf16[1,2,16,32,64]{4,2,3,1,0:T(8,128)(2,1)}, bf16[1,2,16,32,64]{4,2,3,1,0:T(8,128)(2,1)}, u32[]{:S(2)}, u32[]{:S(2)}) collective-permute-start(bf16[1,2,16,32,64]{4,2,3,1,0:T(8,128)(2,1)} %get-tuple-element.11), channel_id=1, source_target_pairs={{0,4},{4,8},{8,12},{1,5},{5,9},{9,13},{2,6},{6,10},{10,14},{3,7},{... | collective-permute-start | bytes 393224 | tf_op jit(solution)/shard_map/ppermute | solution.py:14
  122.4 37.9 %collective-permute-start.3 = (bf16[1,2,16,32,64]{4,2,3,1,0:T(8,128)(2,1)}, bf16[1,2,16,32,64]{4,2,3,1,0:T(8,128)(2,1)}, u32[]{:S(2)}, u32[]{:S(2)}) collective-permute-start(bf16[1,2,16,32,64]{4,2,3,1,0:T(8,128)(2,1)} %get-tuple-element.12), channel_id=1, source_target_pairs={{4,0},{8,4},{12,8},{5,1},{9,5},{13,9},{6,2},{10,6},{14,10},{7,3},{... | collective-permute-start | bytes 393224 | tf_op jit(solution)/shard_map/ppermute | solution.py:15
  160.2 78.4 %reduce-scatter.3.cloned.1.call-start = ((), (), s32[]{:S(2)}) async-start(), calls=%async_computation.3 | async-start | bytes 2621440 | tf_op jit(solution)/shard_map/reduce_scatter | solution.py:58
  162.2 1.5 copy-start.2
  162.3 1.5 copy-start.8
  174.9 2.1 copy-start.3
Sparse Core Ops, SparseCore 0:
  23.6 63.9 all-gather.2
  160.4 32.2 reduce-scatter.4
  195.0 43.5 reduce-scatter.2
